TPU v7x, 128 devices: a whole 4x4x4 slice. The times are simulated.
128 devices in a mesh: dev: 128 (over y, x, z, core).
Axes of the slice: x: 4, y: 4, z: 4, core: 2. Of those that a mesh axis runs over, the one named last changes fastest.
Arguments:
- params: float32 [59, 262144], P(None, 'dev'), as said below
- blocks: int32 [512, 32], P('dev'), may hold values from 0 to 2047, as said below
- counts: int32 [512], P('dev'), may hold values from 4 to 32, as said below
- pixel_grad: float32 [3, 524288], P(None, 'dev'), may hold values from -192 to 192
Outputs:
- param_grad: float32 [59, 262144], P(None, 'dev')
Inputs may be any that keep to these rules, and one draw needn't show every extreme that they name: Block b is owned by device b // 16. Within the tiles of one device no block appears twice, and for every owner exactly 1 of that device's 4 * 32 slots, used or not, name its blocks. `counts`: in every draw all tiles of some one device have 32 used slots. `params`: row 2, the depth, lies from 3 to 6; row 6 from 1 to 2; row 10 below -2.
All inputs are finite; a program needn't handle non-finite values.
Results may differ from a plain program's by a relative error of at most 0.0003.
Values sent between devices are 32-bit elements; how exact they have to be, the bound alone decides.
A program may use at most 128 MiB of HBM per device.

v0:
```python
import jax
import jax.numpy as jnp
from jax import lax
from jax.sharding import PartitionSpec as P

BLOCK = 128
TILE_SIDE = 32
TILES_X = 32


sh_zero = 0.28209479177387814
sh_one = 0.4886025119029199
sh_two = [
    1.0925484305920792,
    -1.0925484305920792,
    0.31539156525252005,
    -1.0925484305920792,
    0.5462742152960396,
]
sh_three = [
    -0.5900435899266435,
    2.890611442640554,
    -0.4570457994644658,
    0.3731763325901154,
    -0.4570457994644658,
    1.445305721320277,
    -0.5900435899266435,
]


def sh_basis(dir_x, dir_y, dir_z):
    sq_x = dir_x * dir_x
    sq_y = dir_y * dir_y
    sq_z = dir_z * dir_z
    return [
        sh_zero + 0.0 * dir_x,
        -sh_one * dir_y,
        sh_one * dir_z,
        -sh_one * dir_x,
        sh_two[0] * dir_x * dir_y,
        sh_two[1] * dir_y * dir_z,
        sh_two[2] * (2.0 * sq_z - sq_x - sq_y),
        sh_two[3] * dir_x * dir_z,
        sh_two[4] * (sq_x - sq_y),
        sh_three[0] * dir_y * (3.0 * sq_x - sq_y),
        sh_three[1] * dir_x * dir_y * dir_z,
        sh_three[2] * dir_y * (4.0 * sq_z - sq_x - sq_y),
        sh_three[3] * dir_z * (2.0 * sq_z - 3.0 * sq_x - 3.0 * sq_y),
        sh_three[4] * dir_x * (4.0 * sq_z - sq_x - sq_y),
        sh_three[5] * dir_z * (sq_x - sq_y),
        sh_three[6] * dir_x * (sq_x - 3.0 * sq_y),
    ]


def screen(params, focal_len, centre_x, centre_y):
    mean_x, mean_y, depths = (params[0], params[1], params[2])
    scales = jnp.exp(params[3:6])
    quat = params[6:10]
    quat = quat / jnp.sqrt(jnp.sum(quat * quat, axis=0))
    quat_r, quat_i, quat_j, quat_k = (quat[0], quat[1], quat[2], quat[3])
    rotation = [
        [
            1.0 - 2.0 * (quat_j * quat_j + quat_k * quat_k),
            2.0 * (quat_i * quat_j - quat_r * quat_k),
            2.0 * (quat_i * quat_k + quat_r * quat_j),
        ],
        [
            2.0 * (quat_i * quat_j + quat_r * quat_k),
            1.0 - 2.0 * (quat_i * quat_i + quat_k * quat_k),
            2.0 * (quat_j * quat_k - quat_r * quat_i),
        ],
        [
            2.0 * (quat_i * quat_k - quat_r * quat_j),
            2.0 * (quat_j * quat_k + quat_r * quat_i),
            1.0 - 2.0 * (quat_i * quat_i + quat_j * quat_j),
        ],
    ]
    inv_z = 1.0 / depths
    diag_jac = focal_len * inv_z
    side_x = -focal_len * mean_x * inv_z * inv_z
    side_y = -focal_len * mean_y * inv_z * inv_z
    upper = [
        (diag_jac * rotation[0][column] + side_x * rotation[2][column]) * scales[column]
        for column in range(3)
    ]
    lower = [
        (diag_jac * rotation[1][column] + side_y * rotation[2][column]) * scales[column]
        for column in range(3)
    ]
    cov_xx = upper[0] * upper[0] + upper[1] * upper[1] + upper[2] * upper[2] + 0.3
    cov_xy = upper[0] * lower[0] + upper[1] * lower[1] + upper[2] * lower[2]
    cov_yy = lower[0] * lower[0] + lower[1] * lower[1] + lower[2] * lower[2] + 0.3
    determ = cov_xx * cov_yy - cov_xy * cov_xy
    screen_u = focal_len * mean_x * inv_z + centre_x
    screen_v = focal_len * mean_y * inv_z + centre_y
    opacity = jax.nn.sigmoid(params[10])
    distance = jnp.sqrt(mean_x * mean_x + mean_y * mean_y + depths * depths)
    basis = sh_basis(mean_x / distance, mean_y / distance, depths / distance)
    colors = [
        0.5
        + sum((basis[harmonic] * params[11 + 16 * channel + harmonic] for harmonic in range(16)))
        for channel in range(3)
    ]
    features = jnp.stack(
        [screen_u, screen_v, cov_yy / determ, -cov_xy / determ, cov_xx / determ, opacity] + colors,
        axis=0,
    )
    return features.reshape(9, -1, BLOCK).transpose(1, 0, 2)


def coords_of(tile_id, positions):
    pix_x = (tile_id % TILES_X * TILE_SIDE + positions % TILE_SIDE).astype(jnp.float32) + 0.5
    pix_y = (tile_id // TILES_X * TILE_SIDE + positions // TILE_SIDE).astype(jnp.float32) + 0.5
    return (pix_x, pix_y)


def pixel_coords(tile_id):
    return coords_of(tile_id, jnp.arange(TILE_SIDE * TILE_SIDE, dtype=jnp.int32))


def pair_terms(feature, pix_x, pix_y):
    off_x = pix_x[:, None] - feature[0][None, :]
    off_y = pix_y[:, None] - feature[1][None, :]
    exponent = (
        -0.5 * (feature[2][None, :] * off_x * off_x + feature[4][None, :] * off_y * off_y)
        - feature[3][None, :] * off_x * off_y
    )
    falloff = jnp.exp(exponent)
    return (off_x, off_y, falloff, feature[5][None, :] * falloff)


def tile_gradients(listed, live_count, cotangent, pix_x, pix_y):
    precise = lax.Precision.HIGHEST
    pixels = pix_x.shape[0]

    def forward(slot_idx, state_in):
        log_trans, colors = state_in
        feature = listed[slot_idx]
        alphas = pair_terms(feature, pix_x, pix_y)[3]
        log_keep = jnp.log(1.0 - alphas)
        before = jnp.cumsum(log_keep, axis=1) - log_keep
        weight = jnp.exp(log_trans[:, None] + before) * alphas
        colors = colors + jnp.dot(weight, feature[6:9].T, precision=precise)
        return (log_trans + jnp.sum(log_keep, axis=1), colors)

    start_state = (jnp.zeros((pixels,), jnp.float32), jnp.zeros((pixels, 3), jnp.float32))
    image = lax.fori_loop(0, live_count, forward, start_state)[1]

    def backward(slot_idx, state_in):
        log_trans, done, gradients = state_in
        feature = listed[slot_idx]
        off_x, off_y, falloff, alphas = pair_terms(feature, pix_x, pix_y)
        log_keep = jnp.log(1.0 - alphas)
        before = jnp.cumsum(log_keep, axis=1) - log_keep
        transmit = jnp.exp(log_trans[:, None] + before)
        weight = transmit * alphas
        dalpha = jnp.zeros_like(alphas)
        for channel in range(3):
            shaded = weight * feature[6 + channel][None, :]
            behind = (image[:, channel] - done[:, channel])[:, None] - jnp.cumsum(shaded, axis=1)
            dalpha = dalpha + cotangent[channel][:, None] * (
                transmit * feature[6 + channel][None, :] - behind / (1.0 - alphas)
            )
        dcolor = jnp.dot(cotangent, weight, precision=precise)
        dpower = dalpha * alphas
        sums_list = [
            jnp.sum(dpower * (feature[2][None, :] * off_x + feature[3][None, :] * off_y), axis=0),
            jnp.sum(dpower * (feature[3][None, :] * off_x + feature[4][None, :] * off_y), axis=0),
            -0.5 * jnp.sum(dpower * off_x * off_x, axis=0),
            -jnp.sum(dpower * off_x * off_y, axis=0),
            -0.5 * jnp.sum(dpower * off_y * off_y, axis=0),
            jnp.sum(dalpha * falloff, axis=0),
        ]
        block_grad = jnp.concatenate([jnp.stack(sums_list, axis=0), dcolor], axis=0)
        gradients = lax.dynamic_update_index_in_dim(gradients, block_grad, slot_idx, 0)
        done = done + jnp.dot(weight, feature[6:9].T, precision=precise)
        return (log_trans + jnp.sum(log_keep, axis=1), done, gradients)

    return lax.fori_loop(
        0, live_count, backward, (start_state[0], start_state[1], jnp.zeros_like(listed))
    )[2]


def body(params, blocks, counts, pixel_grad):
    tiles_dev = counts.shape[0]
    devices = lax.axis_size("dev")
    image_width = TILES_X * TILE_SIDE
    height = devices * tiles_dev // TILES_X * TILE_SIDE
    local_feat, pullback = jax.vjp(
        lambda values: screen(values, float(image_width), image_width / 2.0, height / 2.0), params
    )
    flat_ids = blocks.reshape(-1)
    pixels = TILE_SIDE * TILE_SIDE
    cotangent = pixel_grad.reshape(3, tiles_dev, pixels).transpose(1, 0, 2)
    first_tile = lax.axis_index("dev") * tiles_dev
    all_feat = lax.all_gather(local_feat, "dev", axis=0, tiled=True)

    def one_tile(tile_args):
        tile_num, tile_feat, live_count, tile_cot = tile_args
        pix_x, pix_y = pixel_coords(first_tile + tile_num)
        return tile_gradients(tile_feat, live_count, tile_cot, pix_x, pix_y)

    gradients = lax.map(
        one_tile, (jnp.arange(tiles_dev, dtype=jnp.int32), all_feat[blocks], counts, cotangent)
    )
    dense_grad = jnp.zeros_like(all_feat).at[flat_ids].add(gradients.reshape(-1, 9, BLOCK))
    feature_grad = lax.psum_scatter(dense_grad, "dev", scatter_dimension=0, tiled=True)
    return pullback(feature_grad)[0]


def solution(mesh):
    return jax.shard_map(
        body,
        mesh=mesh,
        in_specs=(P(None, "dev"), P("dev", None), P("dev"), P(None, "dev")),
        out_specs=P(None, "dev"),
        check_vma=False,
    )
```

profile of v0, /device:TPU:1, one launch (start us, length us, event | category | flops | bytes accessed | tf_op | source)
XLA Modules:
  0.0 2036.8 jit_solution(7160727513263844686)
XLA Ops:
  8.3 1.9 add_add_fusion.15
  10.2 1.9 add_add_fusion.16
  12.1 1.8 add_add_fusion.17
  14.9 1.8 fusion.145
  20.1 77.7 %all-gather.2.cloned.1.call-done = f32[2048,9,128]{2,0,1:T(8,128)} async-done(((f32[16,9,128]{2,0,1:T(8,128)}), f32[2048,9,128]{2,0,1:T(8,128)}) %all-gather.2.cloned.1.call-update) | async-done | bytes 9437200 | tf_op jit(solution)/shard_map/all_gather | solution.py:196
  97.7 12.8 copy.7
  110.5 7.4 gather_fusion
  118.4 502.0 %while.67 = (s32[]{:T(128)}, f32[4,32,9,128]{3,2,1,0:T(8,128)}, s32[4]{0:T(128)}, f32[4,32,9,128]{3,2,1,0:T(8,128)}, s32[4]{0:T(128)}, /*index=5*/s32[]{:T(128)}...) while((s32[]{:T(128)}, f32[4,32,9,128]{3,2,1,0:T(8,128)}, ...), condition=%wide.region_19.20_spmd, body=%wide.region_1.19_spmd.sunk | while | flops 113947312 | bytes 16455790 | solution.py:203
  118.4 1.2 dynamic_slice.47
  119.6 1.3 dynamic_slice.48
  123.4 24.7 %while.68 = (s32[]{:T(128)}, f32[1024]{0:T(1024)S(1)}, f32[1024,3]{0,1:T(4,128)S(1)}, s32[]{:T(128)}, f32[32,9,128]{2,1,0:T(8,128)S(1)}, /*index=5*/s32[]{:T(128...) while((s32[]{:T(128)}, f32[1024]{0:T(1024)S(1)}, ...), condition=%wide.region_5.5_spmd.clone, body=%wide.region_2.4_spmd.clone.sunk | while | flops 25318408 | bytes 2185531 | solution.py:147
  148.1 69.4 %while.69 = (s32[]{:T(128)}, f32[1024]{0:T(1024)S(1)}, f32[1024,3]{0,1:T(4,128)S(1)}, f32[32,9,128]{2,1,0:T(8,128)S(1)}, s32[]{:T(128)}, /*index=5*/f32[32,9,128...) while((s32[]{:T(128)}, f32[1024]{0:T(1024)S(1)}, ...), condition=%wide.region_18.18_spmd.clone, body=%wide.region_6.17_spmd.clone.sunk | while | flops 88628880 | bytes 13360023 | solution.py:179
  159.7 1.0 multiply_multiply_fusion.30
  218.3 1.2 dynamic_slice.47
  219.5 1.3 dynamic_slice.48
  223.3 31.9 %while.68 = (s32[]{:T(128)}, f32[1024]{0:T(1024)S(1)}, f32[1024,3]{0,1:T(4,128)S(1)}, s32[]{:T(128)}, f32[32,9,128]{2,1,0:T(8,128)S(1)}, /*index=5*/s32[]{:T(128...) while((s32[]{:T(128)}, f32[1024]{0:T(1024)S(1)}, ...), condition=%wide.region_5.5_spmd.clone, body=%wide.region_2.4_spmd.clone.sunk | while | flops 25318408 | bytes 2185531 | solution.py:147
  255.3 90.1 %while.69 = (s32[]{:T(128)}, f32[1024]{0:T(1024)S(1)}, f32[1024,3]{0,1:T(4,128)S(1)}, f32[32,9,128]{2,1,0:T(8,128)S(1)}, s32[]{:T(128)}, /*index=5*/f32[32,9,128...) while((s32[]{:T(128)}, f32[1024]{0:T(1024)S(1)}, ...), condition=%wide.region_18.18_spmd.clone, body=%wide.region_6.17_spmd.clone.sunk | while | flops 88628880 | bytes 13360023 | solution.py:179
  346.1 1.2 dynamic_slice.47
  347.4 1.3 dynamic_slice.48
  351.1 22.3 %while.68 = (s32[]{:T(128)}, f32[1024]{0:T(1024)S(1)}, f32[1024,3]{0,1:T(4,128)S(1)}, s32[]{:T(128)}, f32[32,9,128]{2,1,0:T(8,128)S(1)}, /*index=5*/s32[]{:T(128...) while((s32[]{:T(128)}, f32[1024]{0:T(1024)S(1)}, ...), condition=%wide.region_5.5_spmd.clone, body=%wide.region_2.4_spmd.clone.sunk | while | flops 25318408 | bytes 2185531 | solution.py:147
  373.4 62.6 %while.69 = (s32[]{:T(128)}, f32[1024]{0:T(1024)S(1)}, f32[1024,3]{0,1:T(4,128)S(1)}, f32[32,9,128]{2,1,0:T(8,128)S(1)}, s32[]{:T(128)}, /*index=5*/f32[32,9,128...) while((s32[]{:T(128)}, f32[1024]{0:T(1024)S(1)}, ...), condition=%wide.region_18.18_spmd.clone, body=%wide.region_6.17_spmd.clone.sunk | while | flops 88628880 | bytes 13360023 | solution.py:179
  436.7 1.2 dynamic_slice.47
  438.0 1.3 dynamic_slice.48
  441.7 46.4 %while.68 = (s32[]{:T(128)}, f32[1024]{0:T(1024)S(1)}, f32[1024,3]{0,1:T(4,128)S(1)}, s32[]{:T(128)}, f32[32,9,128]{2,1,0:T(8,128)S(1)}, /*index=5*/s32[]{:T(128...) while((s32[]{:T(128)}, f32[1024]{0:T(1024)S(1)}, ...), condition=%wide.region_5.5_spmd.clone, body=%wide.region_2.4_spmd.clone.sunk | while | flops 25318408 | bytes 2185531 | solution.py:147
  488.2 131.4 %while.69 = (s32[]{:T(128)}, f32[1024]{0:T(1024)S(1)}, f32[1024,3]{0,1:T(4,128)S(1)}, f32[32,9,128]{2,1,0:T(8,128)S(1)}, s32[]{:T(128)}, /*index=5*/f32[32,9,128...) while((s32[]{:T(128)}, f32[1024]{0:T(1024)S(1)}, ...), condition=%wide.region_18.18_spmd.clone, body=%wide.region_6.17_spmd.clone.sunk | while | flops 88628880 | bytes 13360023 | solution.py:179
  620.4 6.0 broadcast_in_dim.29
  626.4 14.4 scatter_fusion
  640.9 1377.2 %reduce-scatter.2.cloned.1.call-done = f32[16,9,128]{2,1,0:T(8,128)} async-done(((f32[2048,9,128]{2,1,0:T(8,128)}), f32[16,9,128]{2,1,0:T(8,128)}) %reduce-scatter.2.cloned.1.call-update) | async-done | bytes 73744 | tf_op jit(solution)/shard_map/reduce_scatter | solution.py:207
  2018.1 1.1 fusion.118
  2022.9 1.9 fusion.80
  2025.8 1.1 fusion.100
  2027.9 2.0 pad_add_fusion
  (1473 shorter events, 429.2 us)
Async XLA Ops:
  6.5 91.2 %all-gather.2.cloned.1.call-start = ((), (), s32[]{:S(2)}) async-start(), calls=%async_computation.1 | async-start | bytes 9510912 | tf_op jit(solution)/shard_map/all_gather | solution.py:196
  17.8 0.6 copy-start.2
  18.4 1999.6 %reduce-scatter.2.cloned.1.call-start = ((), (), s32[]{:S(2)}) async-start(), calls=%async_computation.2 | async-start | bytes 16908288 | tf_op jit(solution)/shard_map/reduce_scatter | solution.py:207
  620.3 6.1 copy-start.1
  620.3 1399.8 %copy-start.10 = (f32[1,2048]{1,0:T(1,128)S(1)}, f32[1,2048]{1,0:T(1,128)}, u32[]{:S(2)}) copy-start(f32[1,2048]{1,0:T(1,128)} %get-tuple-element.361) | copy-start | bytes 24580
  620.4 1401.8 %copy-start.4 = (f32[1,2048]{1,0:T(1,128)S(1)}, f32[1,2048]{1,0:T(1,128)}, u32[]{:S(2)}) copy-start(f32[1,2048]{1,0:T(1,128)} %get-tuple-element.363) | copy-start | bytes 24580
  620.4 1401.8 %copy-start.5 = (f32[1,2048]{1,0:T(1,128)S(1)}, f32[1,2048]{1,0:T(1,128)}, u32[]{:S(2)}) copy-start(f32[1,2048]{1,0:T(1,128)} %get-tuple-element.365) | copy-start | bytes 24580
  620.4 1401.8 %copy-start.6 = (f32[1,2048]{1,0:T(1,128)S(1)}, f32[1,2048]{1,0:T(1,128)}, u32[]{:S(2)}) copy-start(f32[1,2048]{1,0:T(1,128)} %get-tuple-element.367) | copy-start | bytes 24580
  620.4 1401.8 %copy-start.7 = (f32[1,2048]{1,0:T(1,128)S(1)}, f32[1,2048]{1,0:T(1,128)}, u32[]{:S(2)}) copy-start(f32[1,2048]{1,0:T(1,128)} %get-tuple-element.371) | copy-start | bytes 24580
  620.4 1401.8 %copy-start.8 = (f32[1,2048]{1,0:T(1,128)S(1)}, f32[1,2048]{1,0:T(1,128)}, u32[]{:S(2)}) copy-start(f32[1,2048]{1,0:T(1,128)} %get-tuple-element.374) | copy-start | bytes 24580
  620.4 1401.8 %copy-start.9 = (f32[1,2048]{1,0:T(1,128)S(1)}, f32[1,2048]{1,0:T(1,128)}, u32[]{:S(2)}) copy-start(f32[1,2048]{1,0:T(1,128)} %get-tuple-element.377) | copy-start | bytes 24580
  620.4 1402.2 %copy-start = (f32[59,2048]{1,0:T(8,128)S(1)}, f32[59,2048]{1,0:T(8,128)}, u32[]{:S(2)}) copy-start(f32[59,2048]{1,0:T(8,128)} %param.10) | copy-start | bytes 1449988
  620.4 1402.4 %copy-start.3 = (f32[1,2048]{1,0:T(1,128)S(1)}, f32[1,2048]{1,0:T(1,128)}, u32[]{:S(2)}) copy-start(f32[1,2048]{1,0:T(1,128)} %get-tuple-element.364) | copy-start | bytes 24580
Sparse Core Ops, SparseCore 0:
  18.6 79.1 all-gather.1
  641.0 1377.0 reduce-scatter.1
where the time goes:
time: 2050 us; the launch traced here: 2040 us
  waiting for transfers between devices  1450 us (71%)
  other arithmetic  345 us (17%)
  matrix products  90.7 us (4%)
  loops' own time  73.6 us (4%)
  local copies, waits for them, and re-layouts  58.8 us (3%)
    reduce_scatter x1, waiting for transfers between devices, body(): lax.psum_scatter(dense_grad, 'dev', scatter_dimension=0, tiled=True)  1380 us
    all_gather x1, waiting for transfers between devices, body(): all_feat = lax.all_gather(local_feat, 'dev', axis=0, tiled=True)  77.7 us
    another operation x153, other arithmetic, backward(): jnp.cumsum(shaded, axis=1)  74.4 us
    mul x51, other arithmetic, backward(): dpower = dalpha * alphas  53 us
    reduce_sum x51, other arithmetic, backward(): jnp.sum(dpower * (feature[3][None, :] * off_x + feature[4][None, :] * off...  47.8 us
    dot_general x51, matrix products, forward(): colors = colors + jnp.dot(weight, feature[6:9].T, precision=precise)  43.8 us
  transfers between devices with their start and end apart: 2, of which 2 were waited for; matrix products, arithmetic and copies ran while one was open for 0% of the time, Pallas kernels for 0%

commit v1 on v0

v1 whole, which is shorter than its diff:
```python
import jax
import jax.numpy as jnp
from jax import lax
from jax.experimental import pallas as pl
from jax.experimental.pallas import tpu as pltpu
from jax.sharding import PartitionSpec as P

LOG2E = 1.4426950408889634
sh_zero = 0.28209479177387814
sh_one = 0.4886025119029199
sh_two = [
    1.0925484305920792,
    -1.0925484305920792,
    0.31539156525252005,
    -1.0925484305920792,
    0.5462742152960396,
]
sh_three = [
    -0.5900435899266435,
    2.890611442640554,
    -0.4570457994644658,
    0.3731763325901154,
    -0.4570457994644658,
    1.445305721320277,
    -0.5900435899266435,
]


def sh_basis(dir_x, dir_y, dir_z):
    sq_x = dir_x * dir_x
    sq_y = dir_y * dir_y
    sq_z = dir_z * dir_z
    return [
        sh_zero + 0.0 * dir_x,
        -sh_one * dir_y,
        sh_one * dir_z,
        -sh_one * dir_x,
        sh_two[0] * dir_x * dir_y,
        sh_two[1] * dir_y * dir_z,
        sh_two[2] * (2.0 * sq_z - sq_x - sq_y),
        sh_two[3] * dir_x * dir_z,
        sh_two[4] * (sq_x - sq_y),
        sh_three[0] * dir_y * (3.0 * sq_x - sq_y),
        sh_three[1] * dir_x * dir_y * dir_z,
        sh_three[2] * dir_y * (4.0 * sq_z - sq_x - sq_y),
        sh_three[3] * dir_z * (2.0 * sq_z - 3.0 * sq_x - 3.0 * sq_y),
        sh_three[4] * dir_x * (4.0 * sq_z - sq_x - sq_y),
        sh_three[5] * dir_z * (sq_x - sq_y),
        sh_three[6] * dir_x * (sq_x - 3.0 * sq_y),
    ]


def screen(params, focal_len, centre_x, centre_y):
    mean_x, mean_y, depths = (params[0], params[1], params[2])
    scales = [jnp.exp(params[row]) for row in range(3, 6)]
    quat = params[6:10]
    norm = jnp.sqrt(quat[0] * quat[0] + quat[1] * quat[1] + quat[2] * quat[2] + quat[3] * quat[3])
    quat = [part / norm for part in quat]
    quat_r, quat_i, quat_j, quat_k = (quat[0], quat[1], quat[2], quat[3])
    rotation = [
        [
            1.0 - 2.0 * (quat_j * quat_j + quat_k * quat_k),
            2.0 * (quat_i * quat_j - quat_r * quat_k),
            2.0 * (quat_i * quat_k + quat_r * quat_j),
        ],
        [
            2.0 * (quat_i * quat_j + quat_r * quat_k),
            1.0 - 2.0 * (quat_i * quat_i + quat_k * quat_k),
            2.0 * (quat_j * quat_k - quat_r * quat_i),
        ],
        [
            2.0 * (quat_i * quat_k - quat_r * quat_j),
            2.0 * (quat_j * quat_k + quat_r * quat_i),
            1.0 - 2.0 * (quat_i * quat_i + quat_j * quat_j),
        ],
    ]
    inv_z = 1.0 / depths
    diag_jac = focal_len * inv_z
    side_x = -focal_len * mean_x * inv_z * inv_z
    side_y = -focal_len * mean_y * inv_z * inv_z
    upper = [
        (diag_jac * rotation[0][column] + side_x * rotation[2][column]) * scales[column]
        for column in range(3)
    ]
    lower = [
        (diag_jac * rotation[1][column] + side_y * rotation[2][column]) * scales[column]
        for column in range(3)
    ]
    cov_xx = upper[0] * upper[0] + upper[1] * upper[1] + upper[2] * upper[2] + 0.3
    cov_xy = upper[0] * lower[0] + upper[1] * lower[1] + upper[2] * lower[2]
    cov_yy = lower[0] * lower[0] + lower[1] * lower[1] + lower[2] * lower[2] + 0.3
    determ = cov_xx * cov_yy - cov_xy * cov_xy
    screen_u = focal_len * mean_x * inv_z + centre_x
    screen_v = focal_len * mean_y * inv_z + centre_y
    logit = params[10]
    log_opacity = (logit - jnp.log1p(jnp.exp(logit))) * LOG2E
    distance = jnp.sqrt(mean_x * mean_x + mean_y * mean_y + depths * depths)
    basis = sh_basis(mean_x / distance, mean_y / distance, depths / distance)
    colors = [
        0.5
        + sum((basis[harmonic] * params[11 + 16 * channel + harmonic] for harmonic in range(16)))
        for channel in range(3)
    ]
    return [screen_u, screen_v, cov_yy / determ, -cov_xy / determ, cov_xx / determ, log_opacity] + colors
BLOCK=128; SIDE=32; TX=32; PIX=1024; MAXB=32
f32=jnp.float32; bf16=jnp.bfloat16

def split3(x):
    hi=x.astype(bf16).astype(f32); r=x-hi
    mid=r.astype(bf16).astype(f32); lo=r-mid
    return hi,mid,lo

def tiles_kernel(blocks_ref, counts_ref, feat_ref, cot_ref, out_ref,
                 fs, xs, lhs, rhs, red, eq, al, ws, qs, eb, res):
    first_tile=lax.axis_index("dev")*4
    lane=lax.broadcasted_iota(jnp.int32,(1,PIX),1)
    X=(lane%SIDE-16).astype(f32); Y=(lane//SIDE-16).astype(f32)
    mono=[X*X,X*Y,Y*Y,X,Y,jnp.ones_like(X)]
    out_ref[...]=jnp.zeros_like(out_ref)
    rhs[...]=jnp.zeros_like(rhs)
    for part in range(3):
        for k in range(6): rhs[16*part+k:16*part+k+1,0:PIX]=mono[k]
    eb_zero=None
    def tile(ti,_):
        cnt=counts_ref[ti]
        tid=first_tile+ti
        cx=((tid%TX)*SIDE).astype(f32)+16.5
        cy=((tid//TX)*SIDE).astype(f32)+16.5
        def gat(t,_):
            ow=blocks_ref[ti,t]//16
            for f in range(9): fs[f,pl.ds(t,1),:]=feat_ref[ow,f]
            return 0
        lax.fori_loop(0,cnt,gat,0)
        u=fs[0]-cx; v=fs[1]-cy; A=fs[2]; B=fs[3]; C=fs[4]; lo2=fs[5]
        p=A*u+B*v; r=B*u+C*v
        cf=[(-0.5*LOG2E)*A,(-LOG2E)*B,(-0.5*LOG2E)*C,LOG2E*p,LOG2E*r,(-0.5*LOG2E)*(u*p+v*r)+lo2,
            fs[6],fs[7],fs[8],fs[6],fs[7],fs[8],fs[6],fs[7],fs[8]]
        for k in range(15): xs[:,k,:]=cf[k]
        xs[:,15,:]=jnp.zeros_like(u)
        for c in range(3):
            ct=cot_ref[c:c+1,pl.ds(pl.multiple_of(ti*PIX,PIX),PIX)]
            h,m,l=split3(ct)
            for part in range(3):
                b=16*part+6+c
                rhs[b:b+1,PIX:]=h; rhs[b+3:b+4,PIX:]=m; rhs[b+6:b+7,PIX:]=l
        R=jnp.concatenate([rhs[0:6,0:PIX],rhs[6:15,PIX:],jnp.zeros((1,PIX),f32)],axis=0)
        red[...]=jnp.concatenate([R,jnp.zeros((112,PIX),f32)],axis=0).T.astype(bf16)
        def slotp(t,_):
            x=xs[t]
            h,m,l=split3(x)
            y=jnp.concatenate([h,m,l,jnp.zeros((80,128),f32)],axis=0).T
            for k in range(8):
                mm=t*8+k
                s=mm//cnt; j0=16*(mm%cnt)
                lhs[pl.ds(j0*8+s,16,stride=8),:]=y[16*k:16*k+16,:]
            return 0
        lax.fori_loop(0,cnt,slotp,0)
        rb=rhs[...].astype(bf16)
        def fwd(b,st):
            T,Cc=st
            L=lhs[pl.ds(pl.multiple_of(b*128,128),128),0:48].astype(bf16)
            eq[...]=jnp.dot(L,rb,preferred_element_type=f32)
            for jj in range(16):
                rs=pl.ds(pl.multiple_of(b*128+8*jj,8),8)
                a=jnp.exp2(eq[8*jj:8*jj+8,0:PIX])
                q=eq[8*jj:8*jj+8,PIX:]
                w=T*a; T=T-w; Cc=Cc+w*q
                al[rs,:]=a; ws[rs,:]=w; qs[rs,:]=q
            return T,Cc
        K,Cc=lax.fori_loop(0,cnt,fwd,(jnp.ones((8,PIX),f32),jnp.zeros((8,PIX),f32)))
        P=[jnp.ones((1,PIX),f32)]
        for s in range(7): P.append(P[-1]*K[s:s+1])
        V=[jnp.zeros((1,PIX),f32)]
        for s in range(7,0,-1): V.append(Cc[s:s+1]+K[s:s+1]*V[-1])
        Pv=jnp.concatenate(P,axis=0); V0=jnp.concatenate(V[::-1],axis=0)
        lane128=lax.broadcasted_iota(jnp.int32,(128,128),1)
        def bwd(i,V):
            b=cnt-1-i
            for jp in range(7,-1,-1):
                es=[None,None]; wv=[None,None]
                for h in (1,0):
                    rs=pl.ds(pl.multiple_of(b*128+16*jp+8*h,8),8)
                    d=qs[rs,:]-V
                    w=ws[rs,:]*Pv
                    es[h]=w*d; wv[h]=w
                    V=V+al[rs,:]*d
                e2=jnp.concatenate(es,axis=0); w2=jnp.concatenate(wv,axis=0)
                eh=e2.astype(bf16); wh=w2.astype(bf16)
                eb[16*jp:16*jp+16,:]=eh
                eb[128+16*jp:128+16*jp+16,:]=(e2-eh.astype(f32)).astype(bf16)
                eb[256+16*jp:256+16*jp+16,:]=wh
                eb[384+16*jp:384+16*jp+16,:]=(w2-wh.astype(f32)).astype(bf16)
            rr=jnp.dot(eb[...],red[...],preferred_element_type=f32)
            o=jnp.where(lane128<6,rr[0:128]+rr[128:256],rr[256:384]+rr[384:512])
            res[pl.ds(pl.multiple_of(b*128,128),128),:]=o
            return V
        lax.fori_loop(0,cnt,bwd,V0)
        def slote(t,_):
            ow=blocks_ref[ti,t]//16
            ps=[]
            for k in range(8):
                mm=t*8+k
                s=mm//cnt; j0=16*(mm%cnt)
                ps.append(res[pl.ds(j0*8+s,16,stride=8),:])
            M=jnp.concatenate(ps,axis=0).T[0:16,:]
            row=lambda k: M[k:k+1,:]
            mxx,mxy,myy,mx,my,m1=[row(k) for k in range(6)]
            ff=lambda f: feat_ref[ow,f]
            u=ff(0)-cx; v=ff(1)-cy; A=ff(2); B=ff(3); C=ff(4)
            sx=mx-u*m1; sy=my-v*m1
            sxx=mxx-2.0*u*mx+u*u*m1
            syy=myy-2.0*v*my+v*v*m1
            sxy=mxy-u*my-v*mx+u*v*m1
            o=[A*sx+B*sy,B*sx+C*sy,-0.5*sxx,-sxy,-0.5*syy,m1]+[row(6+c)+row(9+c)+row(12+c) for c in range(3)]
            for f in range(9): out_ref[ow,f]=o[f]
            return 0
        lax.fori_loop(0,cnt,slote,0)
        return 0
    lax.fori_loop(0,4,tile,0)
def tiles(blocks,counts,feat,cot):
    sm=pl.BlockSpec(memory_space=pltpu.SMEM); vm=pl.BlockSpec(memory_space=pltpu.VMEM)
    return pl.pallas_call(tiles_kernel,out_shape=jax.ShapeDtypeStruct((128,9,1,128),f32),
        in_specs=[sm,sm,vm,vm],out_specs=vm,
        scratch_shapes=[pltpu.VMEM((9,32,128),f32),pltpu.VMEM((32,16,128),f32),pltpu.VMEM((4096,128),f32),
            pltpu.VMEM((48,2*PIX),f32),pltpu.VMEM((PIX,128),bf16),pltpu.VMEM((128,2*PIX),f32),
            pltpu.VMEM((4096,PIX),f32),pltpu.VMEM((4096,PIX),f32),pltpu.VMEM((4096,PIX),f32),
            pltpu.VMEM((512,PIX),bf16),pltpu.VMEM((4096,128),f32)],
        compiler_params=pltpu.CompilerParams(vmem_limit_bytes=67043328))(blocks,counts,feat,cot)


def load_params(p_ref):
    return [p_ref[row : row + 1, :].reshape(16, BLOCK) for row in range(59)]


def screen_rows(rows):
    return screen(rows, 1024.0, 512.0, 256.0)


def prep_kernel(idx_ref, p_ref, send_ref, fsc):
    for f, value in enumerate(screen_rows(load_params(p_ref))):
        fsc[f] = jnp.maximum(value, -1000.0) if f == 5 else value

    def put(d, _):
        for f in range(9):
            send_ref[d, f] = fsc[f, pl.ds(idx_ref[d], 1), :]
        return 0

    lax.fori_loop(0, 128, put, 0)


def final_kernel(idx_ref, p_ref, recv_ref, out_ref, acc):
    acc[...] = jnp.zeros_like(acc)

    def add(d, _):
        for f in range(9):
            acc[f, pl.ds(idx_ref[d], 1), :] = acc[f, pl.ds(idx_ref[d], 1), :] + recv_ref[d, f]
        return 0

    lax.fori_loop(0, 128, add, 0)
    pullback = jax.vjp(screen_rows, load_params(p_ref))[1]
    grads = [acc[f] for f in range(9)]
    grads[5] = grads[5] * (1.0 / LOG2E)
    for row, value in enumerate(pullback(grads)[0]):
        out_ref[row : row + 1, :] = value.reshape(1, 2048)


def exchange_kernel(x_ref, o_ref, ssem, rsem, lsem):
    n = lax.axis_size("dev")
    me = lax.axis_index("dev")
    bar = pltpu.get_barrier_semaphore()

    def sig(k, _):
        pl.semaphore_signal(bar, inc=1, device_id=(lax.rem(me + k, n),), device_id_type=pl.DeviceIdType.MESH)
        return 0

    lax.fori_loop(1, n, sig, 0)
    own = pltpu.make_async_copy(x_ref.at[me], o_ref.at[me], lsem)
    own.start()
    pl.semaphore_wait(bar, n - 1)

    def snd(k, _):
        peer = lax.rem(me + k, n)
        pltpu.make_async_remote_copy(
            src_ref=x_ref.at[peer],
            dst_ref=o_ref.at[me],
            send_sem=ssem,
            recv_sem=rsem,
            device_id=(peer,),
            device_id_type=pl.DeviceIdType.MESH,
        ).start()
        return 0

    lax.fori_loop(1, n, snd, 0)
    own.wait()
    most = pl.ds(0, n - 1)
    pltpu.make_async_copy(x_ref.at[most], x_ref.at[most], ssem).wait()
    pltpu.make_async_copy(o_ref.at[most], o_ref.at[most], rsem).wait()


def exchange(x, cid):
    vm = pl.BlockSpec(memory_space=pltpu.VMEM)
    return pl.pallas_call(
        exchange_kernel,
        out_shape=jax.ShapeDtypeStruct(x.shape, x.dtype),
        in_specs=[vm],
        out_specs=vm,
        scratch_shapes=[pltpu.SemaphoreType.DMA] * 3,
        compiler_params=pltpu.CompilerParams(collective_id=cid, has_side_effects=True),
    )(x)


def body(params, blocks, counts, pixel_grad):
    sm = pl.BlockSpec(memory_space=pltpu.SMEM)
    vm = pl.BlockSpec(memory_space=pltpu.VMEM)
    flat = blocks.reshape(-1)
    named = flat[:, None] // 16 == jnp.arange(128, dtype=jnp.int32)[None, :]
    want = jnp.sum(jnp.where(named, flat[:, None] % 16, 0), axis=0)
    asked = lax.all_to_all(want, "dev", 0, 0, tiled=True)
    send = pl.pallas_call(
        prep_kernel,
        out_shape=jax.ShapeDtypeStruct((128, 9, 1, 128), f32),
        in_specs=[sm, vm],
        out_specs=vm,
        scratch_shapes=[pltpu.VMEM((9, 16, 128), f32)],
    )(asked, params)
    feat = exchange(send, 0)
    grads = tiles(blocks, counts, feat, pixel_grad)
    back = exchange(grads, 1)
    return pl.pallas_call(
        final_kernel,
        out_shape=jax.ShapeDtypeStruct((59, 2048), f32),
        in_specs=[sm, vm, vm],
        out_specs=vm,
        scratch_shapes=[pltpu.VMEM((9, 16, 128), f32)],
    )(asked, params, back)


def solution(mesh):
    return jax.shard_map(
        body,
        mesh=mesh,
        in_specs=(P(None, "dev"), P("dev", None), P("dev"), P(None, "dev")),
        out_specs=P(None, "dev"),
        check_vma=False,
    )
```

time: 2050 us -> 212 us (0.10)
  waiting for transfers between devices: 1450 us -> 0 us
  other arithmetic: 345 us -> 3.06 us
  Pallas kernels: 0 us -> 187 us
  matrix products: 90.7 us -> 0 us
  loops' own time: 73.6 us -> 0 us
  local copies, waits for them, and re-layouts: 58.8 us -> 0.88 us
  blocking collectives: 0 us -> 20.7 us
    reduce_scatter x1 -> x0, waiting for transfers between devices: 1380 us -> none  [body(): lax.psum_scatter(dense_grad, 'dev', scatter_dimension=0, tiled=True)]
    pallas_call x0 -> x5, Pallas kernels: none -> 187 us  [the longest x2 111 us: exchange(): pl.pallas_call(exchange_kernel, out_shape=jax.ShapeDtypeStruct(x.shape, x...]
    another operation x255 -> x0, other arithmetic: 124 us -> none  [the longest x153 74.4 us: backward(): jnp.cumsum(shaded, axis=1)]
    mul x268 -> x0, other arithmetic: 93.7 us -> none  [the longest x51 53 us: backward(): dpower = dalpha * alphas]
    dot_general x153 -> x0, matrix products: 90.7 us -> none  [the longest x51 43.8 us: forward(): colors = colors + jnp.dot(weight, feature[6:9].T, precision=precise)]
    all_gather x1 -> x0, waiting for transfers between devices: 77.7 us -> none  [body(): all_feat = lax.all_gather(local_feat, 'dev', axis=0, tiled=True)]
    another operation x9 -> x0, loops' own time: 73.6 us -> none  [the longest x4 37.1 us: tile_gradients(): lax.fori_loop(0, live_count, backward, (start_state[0], start_state[1], j...]
    reduce_sum x53 -> x1, other arithmetic: 48.8 us -> 0.12 us  [body(): want = jnp.sum(jnp.where(named, flat[:, None] % 16, 0), axis=0)]
  transfers between devices with their start and end apart: 2 -> 0, of which waited for: 2 -> 0; matrix products, arithmetic and copies ran while one was open for 0% -> 0% of each run, Pallas kernels for 0% -> 0%
where the time goes in v1:
time: 212 us
  Pallas kernels  187 us (88%)
  blocking collectives  20.7 us (10%)
  other arithmetic  3.06 us (1%)
    pallas_call x2, Pallas kernels, exchange(): pl.pallas_call(exchange_kernel, out_shape=jax.ShapeDtypeStruct(x.shape, x...  111 us
    pallas_call x1, Pallas kernels, tiles(): pl.pallas_call(tiles_kernel, out_shape=jax.ShapeDtypeStruct((128, 9, 1, 1...  64.3 us
    all_to_all x1, blocking collectives, body(): asked = lax.all_to_all(want, 'dev', 0, 0, tiled=True)  20.7 us
    pallas_call x1, Pallas kernels, body(): pl.pallas_call(final_kernel, out_shape=jax.ShapeDtypeStruct((59, 2048), f...  8.5 us

profile of v1, /device:TPU:1, one launch (start us, length us, event | category | flops | bytes accessed | tf_op | source)
XLA Modules:
  0.0 212.1 jit_solution(3386546714802758116)
XLA Ops:
  0.0 0.8 broadcast_in_dim_reshape.4
  0.8 0.1 select_reduce_fusion
  0.9 0.1 copy.7
  1.0 20.7 %all_to_all.11 = s32[128,1,1]{2,1,0:T(1,128)S(1)} all-to-all(s32[128,1,1]{2,1,0:T(1,128)S(1)} %copy.7), channel_id=1, replica_groups=mesh['dev'=128] {'dev'}, dimensions={0} | all-to-all | bytes 1024 | tf_op jit(solution)/shard_map/all_to_all | solution.py:318
  21.7 2.9 %reduce.idx_ref = s32[128]{0:T(128)} reduce(s32[128,1,1]{2,1,0:T(1,128)S(1)} %all_to_all.11, s32[]{:T(128)} %constant.24.clone.1), dimensions={1,2}, to_apply=%all_to_all.8.reduce_sub_computation | reduce | bytes 1028 | tf_op jit(solution)/shard_map/all_to_all | solution.py:318
  24.7 3.3 %shard_map.46.x_ref = f32[128,9,1,128]{3,2,1,0:T(1,128)} custom-call(s32[128]{0:T(128)} %reduce.idx_ref, f32[59,2048]{1,0:T(8,128)} %p_ref.3), custom_call_target="tpu_custom_call" | custom-call | tf_op jit(solution)/shard_map/pallas_call | solution.py:319
  28.0 17.6 %shard_map.47.feat_ref = f32[128,9,1,128]{3,2,1,0:T(1,128)} custom-call(f32[128,9,1,128]{3,2,1,0:T(1,128)} %shard_map.46.x_ref), custom_call_target="tpu_custom_call" | custom-call | tf_op jit(solution)/shard_map/pallas_call | solution.py:302
  45.6 64.3 %shard_map.48.x_ref = f32[128,9,1,128]{3,2,1,0:T(1,128)} custom-call(s32[4,32]{1,0:T(4,128)} %blocks_ref.1, s32[4]{0:T(128)} %counts_ref.1, f32[128,9,1,128]{3,2,1,0:T(1,128)} %shard_map.47.feat_ref, f32[3,4096]{1,0:T(4,128)} %cot_ref.1), custom_call_target="tpu_custom_call" | custom-call | tf_op jit(solution)/shard_map/pallas_call | solution.py:222
  109.8 93.8 %shard_map.49.recv_ref = f32[128,9,1,128]{3,2,1,0:T(1,128)} custom-call(f32[128,9,1,128]{3,2,1,0:T(1,128)} %shard_map.48.x_ref), custom_call_target="tpu_custom_call" | custom-call | tf_op jit(solution)/shard_map/pallas_call | solution.py:302
  203.6 8.5 %shard_map.50 = f32[59,2048]{1,0:T(8,128)} custom-call(s32[128]{0:T(128)} %reduce.idx_ref, f32[59,2048]{1,0:T(8,128)} %p_ref.3, f32[128,9,1,128]{3,2,1,0:T(1,128)} %shard_map.49.recv_ref), custom_call_target="tpu_custom_call" | custom-call | tf_op jit(solution)/shard_map/pallas_call | solution.py:329
  (1 shorter events, 0.0 us)

commit v2 on v1

--- a/solution.py
+++ b/solution.py
@@ -103,6 +103,7 @@
     ]
     return [screen_u, screen_v, cov_yy / determ, -cov_xy / determ, cov_xx / determ, log_opacity] + colors
 BLOCK=128; SIDE=32; TX=32; PIX=1024; MAXB=32
+BU=4; FJ=4; BJ=4
 f32=jnp.float32; bf16=jnp.bfloat16
 
 def split3(x):
@@ -111,7 +112,7 @@
     return hi,mid,lo
 
 def tiles_kernel(blocks_ref, counts_ref, feat_ref, cot_ref, out_ref,
-                 fs, xs, lhs, rhs, red, eq, al, ws, qs, eb, res):
+                 fs, xs, lhs, rhs, wa, wb, pref, vref, st, cots, rbs, al, ws, eA, eB, sbA, zbA, sbB, zbB, res):
     first_tile=lax.axis_index("dev")*4
     lane=lax.broadcasted_iota(jnp.int32,(1,PIX),1)
     X=(lane%SIDE-16).astype(f32); Y=(lane//SIDE-16).astype(f32)
@@ -120,12 +121,23 @@
     rhs[...]=jnp.zeros_like(rhs)
     for part in range(3):
         for k in range(6): rhs[16*part+k:16*part+k+1,0:PIX]=mono[k]
-    eb_zero=None
+    x1=X[:,0:128]; y1=(lax.broadcasted_iota(jnp.int32,(1,128),1)//SIDE-16).astype(f32); o1=jnp.ones_like(x1); z1=jnp.zeros_like(x1)
+    pad=jnp.zeros((80,128),f32)
+    rep=lambda rows: jnp.concatenate([jnp.broadcast_to(x,(8,128)) for x in rows]+[pad],axis=0).T
+    W0=rep([x1*x1,x1*y1,y1*y1,x1,y1,o1])
+    W1=rep([z1,4.0*x1,8.0*y1-16.0,z1,4.0*o1,z1])
+    W2=rep([z1,z1,32.0*o1,z1,z1,z1])
+    wa[...]=jnp.concatenate([W0,W1],axis=0).astype(bf16)
+    wb[...]=jnp.concatenate([W2,W2],axis=0).astype(bf16)
     def tile(ti,_):
         cnt=counts_ref[ti]
         tid=first_tile+ti
         cx=((tid%TX)*SIDE).astype(f32)+16.5
         cy=((tid//TX)*SIDE).astype(f32)+16.5
+        last=128*cnt
+        def step_row(r):
+            r=r+128
+            return jnp.where(r>=last,r-last+1,r)
         def gat(t,_):
             ow=blocks_ref[ti,t]//16
             for f in range(9): fs[f,pl.ds(t,1),:]=feat_ref[ow,f]
@@ -143,88 +155,160 @@
             for part in range(3):
                 b=16*part+6+c
                 rhs[b:b+1,PIX:]=h; rhs[b+3:b+4,PIX:]=m; rhs[b+6:b+7,PIX:]=l
-        R=jnp.concatenate([rhs[0:6,0:PIX],rhs[6:15,PIX:],jnp.zeros((1,PIX),f32)],axis=0)
-        red[...]=jnp.concatenate([R,jnp.zeros((112,PIX),f32)],axis=0).T.astype(bf16)
-        def slotp(t,_):
-            x=xs[t]
-            h,m,l=split3(x)
-            y=jnp.concatenate([h,m,l,jnp.zeros((80,128),f32)],axis=0).T
-            for k in range(8):
-                mm=t*8+k
-                s=mm//cnt; j0=16*(mm%cnt)
-                lhs[pl.ds(j0*8+s,16,stride=8),:]=y[16*k:16*k+16,:]
+        for c in range(3):
+            cots[8*c:8*c+8,:]=jnp.broadcast_to(cot_ref[c:c+1,pl.ds(pl.multiple_of(ti*PIX,PIX),PIX)],(8,PIX))
+        def slotp(tg,row0):
+            for i in range(BU):
+                x=xs[BU*tg+i]
+                h,m,l=split3(x)
+                y=jnp.concatenate([h,m,l,x,jnp.zeros((64,128),f32)],axis=0).T
+                for k in range(8):
+                    lhs[pl.ds(jnp.where(BU*tg+i<cnt,row0,4096),16,stride=8),:]=y[16*k:16*k+16,:]
+                    row0=step_row(row0)
+            return row0
+        lax.fori_loop(0,(cnt+BU-1)//BU,slotp,0)
+        rbs[...]=rhs[...].astype(bf16)
+        def mm(b,h,dst):
+            L=lhs[pl.ds(pl.multiple_of(b*128,128),128),0:48].astype(bf16)
+            dst[...]=jnp.dot(L,rbs[:,h*PIX:h*PIX+PIX],preferred_element_type=f32)
+        def fblock(b,src_):
+            for jg in range(0,16,FJ):
+                rows=[pl.ds(pl.multiple_of(b*128+8*jj,8),8) for jj in range(jg,jg+FJ)]
+                cols=[]
+                for rs in rows:
+                    lrow=lhs[rs,:]
+                    cols.append([jnp.broadcast_to(lrow[:,54+c:55+c],(8,128)) for c in range(3)])
+                for i in range(8):
+                    cs=slice(128*i,128*i+128)
+                    T=st[0:8,cs]; I=[st[8+8*c:16+8*c,cs] for c in range(3)]
+                    for m,rs in enumerate(rows):
+                        aa=jnp.exp2(src_[8*(jg+m):8*(jg+m)+8,cs])
+                        w=T*aa; T=T-w
+                        for c in range(3): I[c]=I[c]+w*cols[m][c]
+                        al[rs,cs]=aa; ws[rs,cs]=w
+                    st[0:8,cs]=T
+                    for c in range(3): st[8+8*c:16+8*c,cs]=I[c]
+        st[0:8,:]=jnp.ones((8,PIX),f32)
+        st[8:32,:]=jnp.zeros((24,PIX),f32)
+        mm(0,0,eA)
+        def fwd(b,_):
+            nb=jnp.minimum(b+1,cnt-1)
+            @pl.when(b%2==0)
+            def _():
+                mm(nb,0,eB); fblock(b,eA)
+            @pl.when(b%2==1)
+            def _():
+                mm(nb,0,eA); fblock(b,eB)
             return 0
-        lax.fori_loop(0,cnt,slotp,0)
-        rb=rhs[...].astype(bf16)
-        def fwd(b,st):
-            T,Cc=st
-            L=lhs[pl.ds(pl.multiple_of(b*128,128),128),0:48].astype(bf16)
-            eq[...]=jnp.dot(L,rb,preferred_element_type=f32)
-            for jj in range(16):
-                rs=pl.ds(pl.multiple_of(b*128+8*jj,8),8)
-                a=jnp.exp2(eq[8*jj:8*jj+8,0:PIX])
-                q=eq[8*jj:8*jj+8,PIX:]
-                w=T*a; T=T-w; Cc=Cc+w*q
-                al[rs,:]=a; ws[rs,:]=w; qs[rs,:]=q
-            return T,Cc
-        K,Cc=lax.fori_loop(0,cnt,fwd,(jnp.ones((8,PIX),f32),jnp.zeros((8,PIX),f32)))
+        lax.fori_loop(0,cnt,fwd,0)
+        K=st[0:8,:]
+        Cc=sum(st[8+8*c:16+8*c,:]*cots[8*c:8*c+8,:] for c in range(3))
         P=[jnp.ones((1,PIX),f32)]
         for s in range(7): P.append(P[-1]*K[s:s+1])
         V=[jnp.zeros((1,PIX),f32)]
         for s in range(7,0,-1): V.append(Cc[s:s+1]+K[s:s+1]*V[-1])
         Pv=jnp.concatenate(P,axis=0); V0=jnp.concatenate(V[::-1],axis=0)
-        lane128=lax.broadcasted_iota(jnp.int32,(128,128),1)
-        def bwd(i,V):
+        pref[...]=Pv
+        lane128=lax.broadcasted_iota(jnp.int32,(8,128),1)//8
+        def sums(sb_,zb_,r0):
+            ra=jnp.dot(sb_[0:256],wa[...],preferred_element_type=f32)
+            rc=jnp.dot(sb_[256:384],wb[...],preferred_element_type=f32)
+            res[pl.ds(pl.multiple_of(r0,8),128),:]=ra[0:128]+ra[128:]+rc+zb_[...]
+        def block(r0,qb,sb_,zb_):
+            for jg in range(16-BJ,-1,-BJ):
+                S=[[None]*3 for _ in range(BJ)]; Z=[[None]*3 for _ in range(BJ)]
+                for i in range(7,-1,-1):
+                    cs=slice(128*i,128*i+128)
+                    V=vref[:,cs]; Pm=pref[:,cs]; ct=[cots[8*c:8*c+8,cs] for c in range(3)]
+                    for m in range(BJ-1,-1,-1):
+                        rs=pl.ds(pl.multiple_of(r0+8*(jg+m),8),8)
+                        d=qb[8*(jg+m):8*(jg+m)+8,cs]-V
+                        w=ws[rs,cs]*Pm
+                        e=w*d
+                        V=V+al[rs,cs]*d
+                        for c in range(3):
+                            zc=w*ct[c]
+                            Z[m][c]=zc if i==7 else Z[m][c]+zc
+                        s=S[m]
+                        if i==7: s[0]=e; s[1]=e; s[2]=e
+                        else:
+                            s[0]=s[0]+e
+                            if i>=1: s[1]=s[1]+s[0]; s[2]=s[2]+s[1]
+                    vref[:,cs]=V
+                for m in range(BJ):
+                    zz=jnp.zeros((8,128),f32)
+                    for c in range(3):
+                        zz=jnp.where(lane128==6+c,jnp.sum(Z[m][c],axis=1,keepdims=True),zz)
+                    zb_[8*(jg+m):8*(jg+m)+8,:]=zz
+                for jp in range(0,BJ,2):
+                    j=8*(jg+jp)
+                    for m in range(3):
+                        x=jnp.concatenate([S[jp][m],S[jp+1][m]],axis=0)
+                        xh=x.astype(bf16); xl=(x-xh.astype(f32)).astype(bf16)
+                        if m<2:
+                            sb_[j:j+16,128*m:128*m+128]=xh
+                            sb_[128+j:128+j+16,128*m:128*m+128]=xl
+                        else:
+                            sb_[256+j:256+j+16,0:128]=xh
+                            sb_[256+j:256+j+16,128:256]=xl
+        vref[...]=V0
+        mm(cnt-1,1,eA)
+        def bwd(i,_):
             b=cnt-1-i
-            for jp in range(7,-1,-1):
-                es=[None,None]; wv=[None,None]
-                for h in (1,0):
-                    rs=pl.ds(pl.multiple_of(b*128+16*jp+8*h,8),8)
-                    d=qs[rs,:]-V
-                    w=ws[rs,:]*Pv
-                    es[h]=w*d; wv[h]=w
-                    V=V+al[rs,:]*d
-                e2=jnp.concatenate(es,axis=0); w2=jnp.concatenate(wv,axis=0)
-                eh=e2.astype(bf16); wh=w2.astype(bf16)
-                eb[16*jp:16*jp+16,:]=eh
-                eb[128+16*jp:128+16*jp+16,:]=(e2-eh.astype(f32)).astype(bf16)
-                eb[256+16*jp:256+16*jp+16,:]=wh
-                eb[384+16*jp:384+16*jp+16,:]=(w2-wh.astype(f32)).astype(bf16)
-            rr=jnp.dot(eb[...],red[...],preferred_element_type=f32)
-            o=jnp.where(lane128<6,rr[0:128]+rr[128:256],rr[256:384]+rr[384:512])
-            res[pl.ds(pl.multiple_of(b*128,128),128),:]=o
-            return V
-        lax.fori_loop(0,cnt,bwd,V0)
-        def slote(t,_):
-            ow=blocks_ref[ti,t]//16
-            ps=[]
-            for k in range(8):
-                mm=t*8+k
-                s=mm//cnt; j0=16*(mm%cnt)
-                ps.append(res[pl.ds(j0*8+s,16,stride=8),:])
-            M=jnp.concatenate(ps,axis=0).T[0:16,:]
-            row=lambda k: M[k:k+1,:]
+            r0=pl.multiple_of(b*128,128)
+            nb=jnp.maximum(b-1,0)
+            @pl.when(i%2==0)
+            def _():
+                mm(nb,1,eB)
+                sums(sbB,zbB,r0+128)
+                block(r0,eA,sbA,zbA)
+            @pl.when(i%2==1)
+            def _():
+                mm(nb,1,eA)
+                sums(sbA,zbA,r0+128)
+                block(r0,eB,sbB,zbB)
+            return 0
+        lax.fori_loop(0,cnt,bwd,0)
+        @pl.when(cnt%2==1)
+        def _(): sums(sbA,zbA,0)
+        @pl.when(cnt%2==0)
+        def _(): sums(sbB,zbB,0)
+        sub=lax.broadcasted_iota(jnp.int32,(16,128),1)%8
+        def slote(tg,row0):
+            M=[None]*8
+            for t in range(8):
+                for k in range(8):
+                    x=res[pl.ds(jnp.minimum(row0,last-1),16,stride=8),:]
+                    M[k]=x if t==0 else jnp.where(sub==t,x,M[k])
+                    row0=step_row(row0)
+            Mt=jnp.concatenate(M,axis=0).T
+            row=lambda k: Mt[8*k:8*k+8,:]
             mxx,mxy,myy,mx,my,m1=[row(k) for k in range(6)]
-            ff=lambda f: feat_ref[ow,f]
-            u=ff(0)-cx; v=ff(1)-cy; A=ff(2); B=ff(3); C=ff(4)
+            tr=pl.ds(pl.multiple_of(8*tg,8),8)
+            u=fs[0,tr,:]-cx; v=fs[1,tr,:]-cy; A=fs[2,tr,:]; B=fs[3,tr,:]; C=fs[4,tr,:]
             sx=mx-u*m1; sy=my-v*m1
             sxx=mxx-2.0*u*mx+u*u*m1
             syy=myy-2.0*v*my+v*v*m1
             sxy=mxy-u*my-v*mx+u*v*m1
-            o=[A*sx+B*sy,B*sx+C*sy,-0.5*sxx,-sxy,-0.5*syy,m1]+[row(6+c)+row(9+c)+row(12+c) for c in range(3)]
-            for f in range(9): out_ref[ow,f]=o[f]
-            return 0
-        lax.fori_loop(0,cnt,slote,0)
+            o=[A*sx+B*sy,B*sx+C*sy,-0.5*sxx,-sxy,-0.5*syy,m1]+[row(6+c) for c in range(3)]
+            for t in range(8):
+                @pl.when(8*tg+t<cnt)
+                def _(t=t):
+                    ow=blocks_ref[ti,8*tg+t]//16
+                    for f in range(9): out_ref[ow,f]=o[f][t:t+1,:]
+            return row0
+        lax.fori_loop(0,(cnt+7)//8,slote,0)
         return 0
     lax.fori_loop(0,4,tile,0)
 def tiles(blocks,counts,feat,cot):
     sm=pl.BlockSpec(memory_space=pltpu.SMEM); vm=pl.BlockSpec(memory_space=pltpu.VMEM)
     return pl.pallas_call(tiles_kernel,out_shape=jax.ShapeDtypeStruct((128,9,1,128),f32),
         in_specs=[sm,sm,vm,vm],out_specs=vm,
-        scratch_shapes=[pltpu.VMEM((9,32,128),f32),pltpu.VMEM((32,16,128),f32),pltpu.VMEM((4096,128),f32),
-            pltpu.VMEM((48,2*PIX),f32),pltpu.VMEM((PIX,128),bf16),pltpu.VMEM((128,2*PIX),f32),
-            pltpu.VMEM((4096,PIX),f32),pltpu.VMEM((4096,PIX),f32),pltpu.VMEM((4096,PIX),f32),
-            pltpu.VMEM((512,PIX),bf16),pltpu.VMEM((4096,128),f32)],
+        scratch_shapes=[pltpu.VMEM((9,32,128),f32),pltpu.VMEM((32,16,128),f32),pltpu.VMEM((4096+128,128),f32),
+            pltpu.VMEM((48,2*PIX),f32),pltpu.VMEM((256,128),bf16),pltpu.VMEM((256,128),bf16),pltpu.VMEM((8,PIX),f32),pltpu.VMEM((8,PIX),f32),
+            pltpu.VMEM((32,PIX),f32),pltpu.VMEM((24,PIX),f32),pltpu.VMEM((48,2*PIX),bf16)]
+            +[pltpu.VMEM((4096,PIX),f32)]*2+[pltpu.VMEM((128,PIX),f32)]*2
+            +[pltpu.VMEM((384,256),bf16),pltpu.VMEM((128,128),f32)]*2+[pltpu.VMEM((4096+128,128),f32)],
         compiler_params=pltpu.CompilerParams(vmem_limit_bytes=67043328))(blocks,counts,feat,cot)
 
 

time: 212 us -> 182 us (0.86)
  Pallas kernels: 187 us -> 157 us
    pallas_call x1, Pallas kernels: 64.3 us -> 48.8 us  [tiles(): pl.pallas_call(tiles_kernel, out_shape=jax.ShapeDtypeStruct((128, 9, 1, 1...]
    pallas_call x2, Pallas kernels: 111 us -> 96.8 us  [exchange(): pl.pallas_call(exchange_kernel, out_shape=jax.ShapeDtypeStruct(x.shape, x...]
where the time goes in v2:
time: 182 us
  Pallas kernels  157 us (86%)
  blocking collectives  20.7 us (11%)
  other arithmetic  3.06 us (2%)
    pallas_call x2, Pallas kernels, exchange(): pl.pallas_call(exchange_kernel, out_shape=jax.ShapeDtypeStruct(x.shape, x...  96.8 us
    pallas_call x1, Pallas kernels, tiles(): pl.pallas_call(tiles_kernel, out_shape=jax.ShapeDtypeStruct((128, 9, 1, 1...  48.8 us
    all_to_all x1, blocking collectives, body(): asked = lax.all_to_all(want, 'dev', 0, 0, tiled=True)  20.7 us
    pallas_call x1, Pallas kernels, body(): pl.pallas_call(final_kernel, out_shape=jax.ShapeDtypeStruct((59, 2048), f...  8.5 us

profile of v2, /device:TPU:1, one launch (start us, length us, event | category | flops | bytes accessed | tf_op | source)
XLA Modules:
  0.0 182.1 jit_solution(4735976070669023710)
XLA Ops:
  0.0 0.8 broadcast_in_dim_reshape.4
  0.8 0.1 select_reduce_fusion
  0.9 0.1 copy.7
  1.0 20.7 %all_to_all.11 = s32[128,1,1]{2,1,0:T(1,128)S(1)} all-to-all(s32[128,1,1]{2,1,0:T(1,128)S(1)} %copy.7), channel_id=1, replica_groups=mesh['dev'=128] {'dev'}, dimensions={0} | all-to-all | bytes 1024 | tf_op jit(solution)/shard_map/all_to_all | solution.py:402
  21.7 2.9 %reduce.idx_ref = s32[128]{0:T(128)} reduce(s32[128,1,1]{2,1,0:T(1,128)S(1)} %all_to_all.11, s32[]{:T(128)} %constant.24.clone.1), dimensions={1,2}, to_apply=%all_to_all.8.reduce_sub_computation | reduce | bytes 1028 | tf_op jit(solution)/shard_map/all_to_all | solution.py:402
  24.7 3.3 %shard_map.46.x_ref = f32[128,9,1,128]{3,2,1,0:T(1,128)} custom-call(s32[128]{0:T(128)} %reduce.idx_ref, f32[59,2048]{1,0:T(8,128)} %p_ref.3), custom_call_target="tpu_custom_call" | custom-call | tf_op jit(solution)/shard_map/pallas_call | solution.py:403
  28.0 17.6 %shard_map.47.feat_ref = f32[128,9,1,128]{3,2,1,0:T(1,128)} custom-call(f32[128,9,1,128]{3,2,1,0:T(1,128)} %shard_map.46.x_ref), custom_call_target="tpu_custom_call" | custom-call | tf_op jit(solution)/shard_map/pallas_call | solution.py:386
  45.6 48.8 %shard_map.48.x_ref = f32[128,9,1,128]{3,2,1,0:T(1,128)} custom-call(s32[4,32]{1,0:T(4,128)} %blocks_ref.1, s32[4]{0:T(128)} %counts_ref.1, f32[128,9,1,128]{3,2,1,0:T(1,128)} %shard_map.47.feat_ref, f32[3,4096]{1,0:T(4,128)} %cot_ref.1), custom_call_target="tpu_custom_call" | custom-call | tf_op jit(solution)/shard_map/pallas_call | solution.py:305
  94.4 79.2 %shard_map.49.recv_ref = f32[128,9,1,128]{3,2,1,0:T(1,128)} custom-call(f32[128,9,1,128]{3,2,1,0:T(1,128)} %shard_map.48.x_ref), custom_call_target="tpu_custom_call" | custom-call | tf_op jit(solution)/shard_map/pallas_call | solution.py:386
  173.6 8.5 %shard_map.50 = f32[59,2048]{1,0:T(8,128)} custom-call(s32[128]{0:T(128)} %reduce.idx_ref, f32[59,2048]{1,0:T(8,128)} %p_ref.3, f32[128,9,1,128]{3,2,1,0:T(1,128)} %shard_map.49.recv_ref), custom_call_target="tpu_custom_call" | custom-call | tf_op jit(solution)/shard_map/pallas_call | solution.py:413
  (1 shorter events, 0.0 us)

commit v3 on v2

--- a/solution.py
+++ b/solution.py
@@ -111,13 +111,25 @@
     mid=r.astype(bf16).astype(f32); lo=r-mid
     return hi,mid,lo
 
-def tiles_kernel(blocks_ref, counts_ref, feat_ref, cot_ref, out_ref,
+def tiles_kernel(ints_ref, feat2_ref, cot2_ref, out2_ref,
                  fs, xs, lhs, rhs, wa, wb, pref, vref, st, cots, rbs, al, ws, eA, eB, sbA, zbA, sbB, zbB, res):
-    first_tile=lax.axis_index("dev")*4
+    me=lax.axis_index("dev")
+    odd=me%2
+    mine=[ints_ref[1,0,k] for k in range(4)]; other=[ints_ref[3,0,k] for k in range(4)]
+    sm_,so_=sum(mine),sum(other)
+    own_full=jnp.logical_or(sm_>so_,jnp.logical_and(sm_==so_,odd==0))
+    full=[jnp.where(own_full,a,b) for a,b in zip(mine,other)]
+    hi_=jnp.maximum(sm_,so_); lo_=jnp.minimum(sm_,so_)
+    best,pick=hi_,jnp.int32(0)
+    for sub in range(1,15):
+        moved=sum(full[k] for k in range(4) if sub>>k&1)
+        top=jnp.maximum(hi_-moved,lo_+moved)
+        better=top<best
+        pick=jnp.where(better,sub,pick); best=jnp.where(better,top,best)
     lane=lax.broadcasted_iota(jnp.int32,(1,PIX),1)
     X=(lane%SIDE-16).astype(f32); Y=(lane//SIDE-16).astype(f32)
     mono=[X*X,X*Y,Y*Y,X,Y,jnp.ones_like(X)]
-    out_ref[...]=jnp.zeros_like(out_ref)
+    out2_ref[...]=jnp.zeros_like(out2_ref)
     rhs[...]=jnp.zeros_like(rhs)
     for part in range(3):
         for k in range(6): rhs[16*part+k:16*part+k+1,0:PIX]=mono[k]
@@ -129,9 +141,18 @@
     W2=rep([z1,z1,32.0*o1,z1,z1,z1])
     wa[...]=jnp.concatenate([W0,W1],axis=0).astype(bf16)
     wb[...]=jnp.concatenate([W2,W2],axis=0).astype(bf16)
-    def tile(ti,_):
-        cnt=counts_ref[ti]
-        tid=first_tile+ti
+    def tile(tx,_):
+        who=tx//4; ti=tx%4
+        gone=jnp.bitwise_and(jnp.right_shift(pick,ti),1)
+        here=jnp.where(own_full,jnp.logical_and(who==0,gone==0),jnp.logical_or(who==0,gone==1))
+        @pl.when(here)
+        def _():
+            one_tile(who,ti)
+        return 0
+    def one_tile(who,ti):
+        feat_ref=feat2_ref.at[who]; cot_ref=cot2_ref.at[who]; out_ref=out2_ref.at[who]
+        cnt=ints_ref[2*who+1,0,ti]
+        tid=jnp.where(who==0,me,me+1-2*odd)*4+ti
         cx=((tid%TX)*SIDE).astype(f32)+16.5
         cy=((tid//TX)*SIDE).astype(f32)+16.5
         last=128*cnt
@@ -139,7 +160,7 @@
             r=r+128
             return jnp.where(r>=last,r-last+1,r)
         def gat(t,_):
-            ow=blocks_ref[ti,t]//16
+            ow=ints_ref[2*who,0,ti*32+t]//16
             for f in range(9): fs[f,pl.ds(t,1),:]=feat_ref[ow,f]
             return 0
         lax.fori_loop(0,cnt,gat,0)
@@ -294,22 +315,22 @@
             for t in range(8):
                 @pl.when(8*tg+t<cnt)
                 def _(t=t):
-                    ow=blocks_ref[ti,8*tg+t]//16
+                    ow=ints_ref[2*who,0,ti*32+8*tg+t]//16
                     for f in range(9): out_ref[ow,f]=o[f][t:t+1,:]
             return row0
         lax.fori_loop(0,(cnt+7)//8,slote,0)
         return 0
-    lax.fori_loop(0,4,tile,0)
-def tiles(blocks,counts,feat,cot):
+    lax.fori_loop(0,8,tile,0)
+def tiles(ints,feat,cot):
     sm=pl.BlockSpec(memory_space=pltpu.SMEM); vm=pl.BlockSpec(memory_space=pltpu.VMEM)
-    return pl.pallas_call(tiles_kernel,out_shape=jax.ShapeDtypeStruct((128,9,1,128),f32),
-        in_specs=[sm,sm,vm,vm],out_specs=vm,
+    return pl.pallas_call(tiles_kernel,out_shape=jax.ShapeDtypeStruct((2,128,9,1,128),f32),
+        in_specs=[sm,vm,vm],out_specs=vm,
         scratch_shapes=[pltpu.VMEM((9,32,128),f32),pltpu.VMEM((32,16,128),f32),pltpu.VMEM((4096+128,128),f32),
             pltpu.VMEM((48,2*PIX),f32),pltpu.VMEM((256,128),bf16),pltpu.VMEM((256,128),bf16),pltpu.VMEM((8,PIX),f32),pltpu.VMEM((8,PIX),f32),
             pltpu.VMEM((32,PIX),f32),pltpu.VMEM((24,PIX),f32),pltpu.VMEM((48,2*PIX),bf16)]
             +[pltpu.VMEM((4096,PIX),f32)]*2+[pltpu.VMEM((128,PIX),f32)]*2
             +[pltpu.VMEM((384,256),bf16),pltpu.VMEM((128,128),f32)]*2+[pltpu.VMEM((4096+128,128),f32)],
-        compiler_params=pltpu.CompilerParams(vmem_limit_bytes=67043328))(blocks,counts,feat,cot)
+        compiler_params=pltpu.CompilerParams(vmem_limit_bytes=67043328))(ints,feat,cot)
 
 
 def load_params(p_ref):
@@ -320,103 +341,175 @@
     return screen(rows, 1024.0, 512.0, 256.0)
 
 
-def prep_kernel(idx_ref, p_ref, send_ref, fsc):
+def everyone(me, n, act):
+    def step(k, _):
+        act(lax.rem(me + k, n))
+        return 0
+
+    lax.fori_loop(1, n, step, 0)
+
+
+def send(src, dst, ssem, rsem, peer):
+    return pltpu.make_async_remote_copy(
+        src_ref=src,
+        dst_ref=dst,
+        send_sem=ssem,
+        recv_sem=rsem,
+        device_id=(peer,),
+        device_id_type=pl.DeviceIdType.MESH,
+    )
+
+
+def all_but_one(ref, sem):
+    rest = ref.at[pl.ds(0, ref.shape[0] - 1)]
+    return pltpu.make_async_copy(rest, rest, sem)
+
+
+def greet(me, n):
+    bar = pltpu.get_barrier_semaphore()
+    everyone(
+        me,
+        n,
+        lambda peer: pl.semaphore_signal(bar, inc=1, device_id=(peer,), device_id_type=pl.DeviceIdType.MESH),
+    )
+    return bar
+
+
+def forward_kernel(ints_ref, p_ref, cot_ref, pair_ref, feat_ref, cot2_ref, idx_ref, lists, fsc, outbox, idxs, sems):
+    n = lax.axis_size("dev")
+    me = lax.axis_index("dev")
+    partner = me + 1 - 2 * lax.rem(me, 2)
+    bar = greet(me, n)
+    own_list = pltpu.make_async_copy(ints_ref.at[0], lists.at[me], sems.at[0])
+    own_ints = pltpu.make_async_copy(ints_ref, pair_ref.at[pl.ds(0, 2)], sems.at[1])
+    own_cot = pltpu.make_async_copy(cot_ref, cot2_ref.at[0], sems.at[2])
+    own_list.start()
+    own_ints.start()
+    own_cot.start()
     for f, value in enumerate(screen_rows(load_params(p_ref))):
         fsc[f] = jnp.maximum(value, -1000.0) if f == 5 else value
+    pl.semaphore_wait(bar, n - 1)
+    everyone(me, n, lambda peer: send(ints_ref.at[0], lists.at[me], sems.at[3], sems.at[4], peer).start())
+    pair_ints = send(ints_ref, pair_ref.at[pl.ds(2, 2)], sems.at[5], sems.at[6], partner)
+    pair_cot = send(cot_ref, cot2_ref.at[1], sems.at[7], sems.at[8], partner)
+    pair_ints.start()
+    pair_cot.start()
+    own_list.wait()
+    all_but_one(lists, sems.at[4]).wait()
+    flat = lists[...].reshape(128, 128)
+    asked = jnp.sum(jnp.where(flat >> 4 == me, flat & 15, 0).astype(f32), axis=1, keepdims=True)
+    idx_ref[...] = jnp.broadcast_to(asked, (128, 128)).T[0:1].astype(jnp.int32)
+    to_scalar = pltpu.make_async_copy(idx_ref, idxs, sems.at[9])
+    to_scalar.start()
+    to_scalar.wait()
 
     def put(d, _):
         for f in range(9):
-            send_ref[d, f] = fsc[f, pl.ds(idx_ref[d], 1), :]
+            outbox[d, f] = fsc[f, pl.ds(idxs[0, d] & 15, 1), :]
         return 0
 
     lax.fori_loop(0, 128, put, 0)
-
-
-def final_kernel(idx_ref, p_ref, recv_ref, out_ref, acc):
-    acc[...] = jnp.zeros_like(acc)
+    own_feat = pltpu.make_async_copy(outbox.at[me], feat_ref.at[0, me], sems.at[10])
+    own_feat.start()
+    everyone(me, n, lambda peer: send(outbox.at[peer], feat_ref.at[0, me], sems.at[11], sems.at[12], peer).start())
+    all_but_one(lists, sems.at[3]).wait()
+    own_ints.wait()
+    own_cot.wait()
+    own_feat.wait()
+    pair_ints.wait()
+    pair_cot.wait()
+    all_but_one(outbox, sems.at[12]).wait()
+    pair_feat = send(feat_ref.at[0], feat_ref.at[1], sems.at[13], sems.at[14], partner)
+    pair_feat.start()
+    all_but_one(outbox, sems.at[11]).wait()
+    pair_feat.wait()
+
+
+def back_kernel(grad_ref, recv_ref, theirs, outbox, sems):
+    n = lax.axis_size("dev")
+    me = lax.axis_index("dev")
+    partner = me + 1 - 2 * lax.rem(me, 2)
+    bar = greet(me, n)
+    pl.semaphore_wait(bar, n - 1)
+    pair = send(grad_ref.at[1], theirs, sems.at[0], sems.at[1], partner)
+    pair.start()
+    pair.wait_recv()
 
     def add(d, _):
         for f in range(9):
-            acc[f, pl.ds(idx_ref[d], 1), :] = acc[f, pl.ds(idx_ref[d], 1), :] + recv_ref[d, f]
+            outbox[d, f] = grad_ref[0, d, f] + theirs[d, f]
         return 0
 
     lax.fori_loop(0, 128, add, 0)
+    own = pltpu.make_async_copy(outbox.at[me], recv_ref.at[me], sems.at[2])
+    own.start()
+    everyone(me, n, lambda peer: send(outbox.at[peer], recv_ref.at[me], sems.at[3], sems.at[4], peer).start())
+    pair.wait_send()
+    own.wait()
+    all_but_one(outbox, sems.at[3]).wait()
+    all_but_one(recv_ref, sems.at[4]).wait()
+
+
+def final_kernel(idx_ref, p_ref, recv_ref, out_ref):
+    rows = lax.broadcasted_iota(jnp.int32, (16, BLOCK), 0)
+
+    def add(d, acc):
+        hit = rows == idx_ref[0, d]
+        return tuple(
+            acc[f] + jnp.where(hit, jnp.broadcast_to(recv_ref[d, f], (16, BLOCK)), 0.0) for f in range(9)
+        )
+
+    zeros = tuple(jnp.zeros((16, BLOCK), f32) for _ in range(9))
+    grads = list(lax.fori_loop(0, 128, add, zeros, unroll=4))
     pullback = jax.vjp(screen_rows, load_params(p_ref))[1]
-    grads = [acc[f] for f in range(9)]
     grads[5] = grads[5] * (1.0 / LOG2E)
     for row, value in enumerate(pullback(grads)[0]):
         out_ref[row : row + 1, :] = value.reshape(1, 2048)
 
 
-def exchange_kernel(x_ref, o_ref, ssem, rsem, lsem):
-    n = lax.axis_size("dev")
-    me = lax.axis_index("dev")
-    bar = pltpu.get_barrier_semaphore()
-
-    def sig(k, _):
-        pl.semaphore_signal(bar, inc=1, device_id=(lax.rem(me + k, n),), device_id_type=pl.DeviceIdType.MESH)
-        return 0
-
-    lax.fori_loop(1, n, sig, 0)
-    own = pltpu.make_async_copy(x_ref.at[me], o_ref.at[me], lsem)
-    own.start()
-    pl.semaphore_wait(bar, n - 1)
-
-    def snd(k, _):
-        peer = lax.rem(me + k, n)
-        pltpu.make_async_remote_copy(
-            src_ref=x_ref.at[peer],
-            dst_ref=o_ref.at[me],
-            send_sem=ssem,
-            recv_sem=rsem,
-            device_id=(peer,),
-            device_id_type=pl.DeviceIdType.MESH,
-        ).start()
-        return 0
-
-    lax.fori_loop(1, n, snd, 0)
-    own.wait()
-    most = pl.ds(0, n - 1)
-    pltpu.make_async_copy(x_ref.at[most], x_ref.at[most], ssem).wait()
-    pltpu.make_async_copy(o_ref.at[most], o_ref.at[most], rsem).wait()
-
-
-def exchange(x, cid):
-    vm = pl.BlockSpec(memory_space=pltpu.VMEM)
-    return pl.pallas_call(
-        exchange_kernel,
-        out_shape=jax.ShapeDtypeStruct(x.shape, x.dtype),
-        in_specs=[vm],
-        out_specs=vm,
-        scratch_shapes=[pltpu.SemaphoreType.DMA] * 3,
-        compiler_params=pltpu.CompilerParams(collective_id=cid, has_side_effects=True),
-    )(x)
-
-
 def body(params, blocks, counts, pixel_grad):
     sm = pl.BlockSpec(memory_space=pltpu.SMEM)
     vm = pl.BlockSpec(memory_space=pltpu.VMEM)
-    flat = blocks.reshape(-1)
-    named = flat[:, None] // 16 == jnp.arange(128, dtype=jnp.int32)[None, :]
-    want = jnp.sum(jnp.where(named, flat[:, None] % 16, 0), axis=0)
-    asked = lax.all_to_all(want, "dev", 0, 0, tiled=True)
-    send = pl.pallas_call(
-        prep_kernel,
-        out_shape=jax.ShapeDtypeStruct((128, 9, 1, 128), f32),
-        in_specs=[sm, vm],
+    block_sums = jax.ShapeDtypeStruct((128, 9, 1, 128), f32)
+    ints = jnp.stack([blocks.reshape(1, 128), jnp.pad(counts, (0, 124)).reshape(1, 128)])
+    pair, feat, cot, idx = pl.pallas_call(
+        forward_kernel,
+        out_shape=[
+            jax.ShapeDtypeStruct((4, 1, 128), jnp.int32),
+            jax.ShapeDtypeStruct((2, 128, 9, 1, 128), f32),
+            jax.ShapeDtypeStruct((2, 3, 4096), f32),
+            jax.ShapeDtypeStruct((1, 128), jnp.int32),
+        ],
+        in_specs=[vm, vm, vm],
+        out_specs=[vm, vm, vm, vm],
+        scratch_shapes=[
+            pltpu.VMEM((128, 1, 128), jnp.int32),
+            pltpu.VMEM((9, 16, 128), f32),
+            pltpu.VMEM((128, 9, 1, 128), f32),
+            pltpu.SMEM((1, 128), jnp.int32),
+            pltpu.SemaphoreType.DMA((15,)),
+        ],
+        compiler_params=pltpu.CompilerParams(collective_id=0, has_side_effects=True),
+    )(ints, params, pixel_grad)
+    grads = tiles(pair, feat, cot)
+    back = pl.pallas_call(
+        back_kernel,
+        out_shape=block_sums,
+        in_specs=[vm],
         out_specs=vm,
-        scratch_shapes=[pltpu.VMEM((9, 16, 128), f32)],
-    )(asked, params)
-    feat = exchange(send, 0)
-    grads = tiles(blocks, counts, feat, pixel_grad)
-    back = exchange(grads, 1)
+        scratch_shapes=[
+            pltpu.VMEM((128, 9, 1, 128), f32),
+            pltpu.VMEM((128, 9, 1, 128), f32),
+            pltpu.SemaphoreType.DMA((5,)),
+        ],
+        compiler_params=pltpu.CompilerParams(collective_id=1, has_side_effects=True),
+    )(grads)
     return pl.pallas_call(
         final_kernel,
         out_shape=jax.ShapeDtypeStruct((59, 2048), f32),
         in_specs=[sm, vm, vm],
         out_specs=vm,
-        scratch_shapes=[pltpu.VMEM((9, 16, 128), f32)],
-    )(asked, params, back)
+    )(idx, params, back)
 
 
 def solution(mesh):

time: 182 us -> 145 us (0.80)
  blocking collectives: 20.7 us -> 0 us
  Pallas kernels: 157 us -> 142 us
  other arithmetic: 3.06 us -> 0.57 us
    all_to_all x1 -> x0, blocking collectives: 20.7 us -> none  [body(): asked = lax.all_to_all(want, 'dev', 0, 0, tiled=True)]
    pallas_call x4 -> x3, Pallas kernels: 149 us -> 139 us  [the longest x1 66.9 us: body(): pl.pallas_call(back_kernel, out_shape=block_sums, in_specs=[vm], out_spec...]
    pallas_call x1, Pallas kernels: 8.5 us -> 3.28 us  [body(): pl.pallas_call(final_kernel, out_shape=jax.ShapeDtypeStruct((59, 2048), f...]
    all_to_all x1 -> x0, other arithmetic: 2.93 us -> none  [body(): asked = lax.all_to_all(want, 'dev', 0, 0, tiled=True)]
where the time goes in v3:
time: 145 us; the launch traced here: 144 us
  Pallas kernels  142 us (98%)
    pallas_call x1, Pallas kernels, body(): pl.pallas_call(back_kernel, out_shape=block_sums, in_specs=[vm], out_spec...  66.9 us
    pallas_call x1, Pallas kernels, tiles(): pl.pallas_call(tiles_kernel, out_shape=jax.ShapeDtypeStruct((2, 128, 9, 1...  38 us
    pallas_call x1, Pallas kernels, body(): pl.pallas_call(forward_kernel, out_shape=[jax.ShapeDtypeStruct((4, 1, 128...  33.9 us
    pallas_call x1, Pallas kernels, body(): pl.pallas_call(final_kernel, out_shape=jax.ShapeDtypeStruct((59, 2048), f...  3.28 us

profile of v3, /device:TPU:1, one launch (start us, length us, event | category | flops | bytes accessed | tf_op | source)
XLA Modules:
  0.0 144.0 jit_solution(5200653349276516095)
XLA Ops:
  0.0 0.8 stack_reshape.6
  0.8 0.7 pad_bitcast_fusion
  1.4 0.6 pad_add_fusion.ints_ref
  2.0 33.9 %shard_map.46 = (s32[4,1,128]{2,1,0:T(1,128)}, f32[2,128,9,1,128]{4,3,2,1,0:T(1,128)}, f32[2,3,4096]{2,1,0:T(4,128)}, s32[1,128]{1,0:T(1,128)}) custom-call(s32[2,1,128]{2,1,0:T(1,128)} %pad_add_fusion.ints_ref, f32[59,2048]{1,0:T(8,128)} %p_ref.3, f32[3,4096]{1,0:T(4,128)} %cot_ref.1), custom_call_target="tpu_custom_call" | custom-call | tf_op jit(solution)/shard_map/pallas_call | solution.py:475
  35.9 38.0 %shard_map.47.grad_ref = f32[2,128,9,1,128]{4,3,2,1,0:T(1,128)} custom-call(s32[4,1,128]{2,1,0:T(1,128)} %get-tuple-element.10.ints_ref, f32[2,128,9,1,128]{4,3,2,1,0:T(1,128)} %get-tuple-element.11.feat2_ref, f32[2,3,4096]{2,1,0:T(4,128)} %get-tuple-element.12.cot2_ref), custom_call_target="tpu_custom_call" | custom-call | tf_op jit(solution)/shard_map/pallas_call | solution.py:326
  73.8 66.9 %shard_map.48.recv_ref = f32[128,9,1,128]{3,2,1,0:T(1,128)} custom-call(f32[2,128,9,1,128]{4,3,2,1,0:T(1,128)} %shard_map.47.grad_ref), custom_call_target="tpu_custom_call" | custom-call | tf_op jit(solution)/shard_map/pallas_call | solution.py:495
  140.7 3.3 %shard_map.49 = f32[59,2048]{1,0:T(8,128)} custom-call(s32[1,128]{1,0:T(1,128)} %get-tuple-element.9.idx_ref, f32[59,2048]{1,0:T(8,128)} %p_ref.3, f32[128,9,1,128]{3,2,1,0:T(1,128)} %shard_map.48.recv_ref), custom_call_target="tpu_custom_call" | custom-call | tf_op jit(solution)/shard_map/pallas_call | solution.py:507
